TPU v7x, 256 devices: a whole 4x4x8 slice. The times are simulated.
256 devices in a mesh: sens: 16 (over z, y_lo), unk: 16 (over x, y_hi, core).
Axes of the slice: x: 4, y: 4 (y_hi: 2, y_lo: 2; y = y_hi * 2 + y_lo), z: 8, core: 2. Of those that a mesh axis runs over, the one named last changes fastest.
Arguments:
- signals: float32 [512, 4, 256], P('sens', None, 'unk'), may hold values from -6 to 6
- kernel: float32 [512, 32, 16384], P('sens', None, 'unk'), may hold values from -0.0234375 to 0.0234375
- tap_weights: float32 [17, 16384], P(None, 'unk'), may hold values from -1.5 to 1.5
Outputs:
- hessian_action: float32 [512, 4, 256], P('sens', None, 'unk')
All inputs are finite; a program needn't handle non-finite values.
Results may differ from a plain program's by a relative error of at most 0.00008.
Values sent between devices are 32-bit elements; how exact they have to be, the bound alone decides.
No kernel may reach another device: no remote copies, remote signals or barrier semaphores. Data moves between devices by JAX's collectives and lax.ppermute only.
A program may use at most 64 MiB of HBM per device.

v0:
```python
import functools

import jax
import jax.numpy as jnp
from jax import lax
from jax.experimental import pallas as pl
from jax.experimental.pallas import tpu as pltpu
from jax.sharding import Mesh, PartitionSpec as P


UNK = ("x", "yh", "c")
PAIRS = ((4, 0), (3, 5), (2, 6), (1, 7))


def ring(size, step):
    return [(i, (i + step) % size) for i in range(size)]


def swap(value, axis):
    return lax.ppermute(value, axis, [(0, 1), (1, 0)])


def split(value):
    high = value.astype(jnp.bfloat16)
    return high, (value - high.astype(jnp.float32)).astype(jnp.bfloat16)


def mirror(steps):
    row = lax.broadcasted_iota(jnp.int32, (steps, steps), 0)
    column = lax.broadcasted_iota(jnp.int32, (steps, steps), 1)
    return jnp.where(row + column == steps - 1, 1.0, 0.0)


VMEM = pl.BlockSpec(memory_space=pltpu.VMEM)


def room(mebibytes):
    return pltpu.CompilerParams(vmem_limit_bytes=mebibytes * 2**20)


def resident(value):
    return pltpu.with_memory_space_constraint(value, pltpu.VMEM)


def skewed(tile):
    lane = lax.broadcasted_iota(jnp.int32, tile.shape, 1)
    row = lax.broadcasted_iota(jnp.int32, tile.shape, 0)
    return jnp.where(lane >= row, pltpu.roll(tile, 0, 1, stride=1, stride_axis=0), 0.0)


def window_kernel(series_ref, high_ref, low_ref, rows_ref, *, group, vectors, lags, steps):
    rows_ref[...] = lax.dot_general(
        series_ref[...], mirror(steps), (((0,), (0,)), ((), ())),
        precision=lax.Precision.HIGHEST,
    )

    def body(block, carry):
        for s in range(group):
            sensor = block * group + s
            for b in range(vectors):
                row = rows_ref[pl.ds(sensor * vectors + b, 1), :]
                here = pl.ds(pl.multiple_of(sensor * lags, lags), lags)
                place = (here, slice(b * steps, (b + 1) * steps))
                high_ref[place], low_ref[place] = split(
                    skewed(jnp.broadcast_to(row, (lags, steps)))
                )
        return carry

    lax.fori_loop(0, rows_ref.shape[0] // (vectors * group), body, 0)


def window_of(series, lags, vectors):
    steps, columns = series.shape
    sensors = columns // vectors
    return pl.pallas_call(
        functools.partial(window_kernel, group=4, vectors=vectors, lags=lags, steps=steps),
        out_shape=[pltpu.VMEM((sensors * lags, vectors * steps), jnp.bfloat16)] * 2,
        in_specs=[VMEM],
        out_specs=[VMEM] * 2,
        scratch_shapes=[pltpu.VMEM((columns, steps), jnp.float32)],
        compiler_params=room(4),
        name="window",
    )(resident(series))


def pair_kernel(scalars_ref, kernel_ref, *refs, lanes):
    *out_refs, half_ref, arrived = refs
    half, z = scalars_ref[0], scalars_ref[1]
    slots = 2 * len(PAIRS)
    slot = lanes // 2
    rows, width = half_ref.shape
    blocks = arrived.shape[0]
    block = rows // blocks
    columns = pl.ds(pl.multiple_of(half * width, width), width)

    def copy_of(i):
        here = pl.ds(pl.multiple_of(i * block, block), block)
        return pltpu.make_async_copy(
            kernel_ref.at[here, columns], half_ref.at[here, :], arrived.at[i]
        )

    for i in range(blocks):
        copy_of(i).start()
    lane = lax.broadcasted_iota(jnp.int32, (block, lanes), 1)

    def body(i, carry):
        copy_of(i).wait()
        here = pl.ds(pl.multiple_of(i * block, block), block)

        def half_of(offset, high):
            place = lax.rem(z + offset, slots)
            start = pl.multiple_of(place // 2 * lanes, lanes)
            shift = lax.rem(lax.rem(place, 2) + high, 2) * slot
            return pltpu.roll(half_ref[here, pl.ds(start, lanes)], shift, 1)

        pairs = iter(PAIRS)
        for out_ref in out_refs:
            for start in range(0, out_ref.shape[1], lanes):
                low, high = next(pairs)
                out_ref[here, start : start + lanes] = jnp.where(
                    lane < slot, half_of(low, 0), half_of(high, 1)
                )
        return carry

    lax.fori_loop(0, blocks, body, 0)


def pairs_of(matrix, half, z, outputs):
    rows, unknowns = matrix.shape
    width = unknowns // 2
    blocks = 8
    return pl.pallas_call(
        functools.partial(pair_kernel, lanes=width // len(PAIRS)),
        out_shape=[pltpu.VMEM((rows, width // outputs), jnp.float32)] * outputs,
        in_specs=[
            pl.BlockSpec(memory_space=pltpu.SMEM),
            pl.BlockSpec(memory_space=pltpu.HBM),
        ],
        out_specs=[VMEM] * outputs,
        scratch_shapes=[
            pltpu.VMEM((rows, width), jnp.float32),
            pltpu.SemaphoreType.DMA((blocks,)),
        ],
        compiler_params=room(4),
        name="pairs",
    )(
        jnp.stack([half, z]).astype(jnp.int32),
        pltpu.with_memory_space_constraint(matrix, pltpu.HBM),
    )


def three_pass(high, low, right_high, right_low):
    dot = functools.partial(jnp.dot, preferred_element_type=jnp.float32)
    rows = high.shape[0]
    both = dot(jnp.concatenate([high, low]), right_high)
    return both[:rows] + both[rows:] + dot(high, right_low)


def adjoint_kernel(
    kept_ref, given_ref, kept_high_ref, kept_low_ref, given_high_ref, given_low_ref, out_ref,
    *, first, block,
):
    out_ref[...] = jnp.zeros(out_ref.shape, jnp.float32)
    width = given_ref.shape[1]

    def body(i, carry):
        here = pl.ds(pl.multiple_of(i * block, block), block)
        kept = split(kept_ref[here, first : first + width].T)
        given = split(given_ref[here, :].T)
        out_ref[...] += three_pass(
            *kept, kept_high_ref[here, :], kept_low_ref[here, :]
        ) + three_pass(*given, given_high_ref[here, :], given_low_ref[here, :])
        return carry

    lax.fori_loop(0, given_ref.shape[0] // block, body, 0)


def adjoint_of(kept, first, given, own_window, other_window):
    operands = [resident(value) for value in (kept, given, *own_window, *other_window)]
    return pl.pallas_call(
        functools.partial(adjoint_kernel, first=first, block=256),
        out_shape=pltpu.VMEM((given.shape[1], own_window[0].shape[1]), jnp.float32),
        in_specs=[VMEM] * len(operands),
        out_specs=VMEM,
        compiler_params=room(8),
        name="adjoint",
    )(*operands)


def early_kernel(*refs, parts):
    out_ref, high_ref, low_ref = refs[-3:]
    fill(high_ref, low_ref, refs[:parts])
    block = 256

    def body(i, carry):
        here = pl.ds(pl.multiple_of(i * block, block), block)
        high, low = split(jnp.concatenate([ref[here, :] for ref in refs[parts:-3]], axis=1))
        out_ref[here, :] = three_pass(high, low, high_ref[...], low_ref[...])
        return carry

    lax.fori_loop(0, out_ref.shape[0] // block, body, 0)


def early_of(kernels, parts):
    width = sum(kernel.shape[1] for kernel in kernels)
    columns = parts[0].shape[1]
    operands = [resident(value) for value in (*parts, *kernels)]
    return pl.pallas_call(
        functools.partial(early_kernel, parts=len(parts)),
        out_shape=pltpu.VMEM((kernels[0].shape[0], columns), jnp.float32),
        in_specs=[VMEM] * len(operands),
        out_specs=VMEM,
        scratch_shapes=[pltpu.VMEM((width, columns), jnp.bfloat16)] * 2,
        compiler_params=room(8),
        name="early",
    )(*operands)


def fill(high_ref, low_ref, parts):
    start = 0
    for part in parts:
        here = slice(start, start + part.shape[0])
        high_ref[here, :], low_ref[here, :] = split(part[...])
        start += part.shape[0]


def forward_kernel(*refs, parts, group, vectors, lags, steps):
    before_ref, out_ref, high_ref, low_ref, product_ref, rows_ref = refs[-6:]
    blocks = before_ref.shape[0] // (group * lags)
    fill(high_ref, low_ref, refs[:parts])

    def multiply(block):
        here = pl.ds(pl.multiple_of(block * group * lags, group * lags), group * lags)
        high, low = split(jnp.concatenate([ref[here, :] for ref in refs[parts:-6]], axis=1))
        product_ref[lax.rem(block, 2)] = before_ref[here, :] + three_pass(
            high, low, high_ref[...], low_ref[...]
        )

    def shear(block):
        for s in range(group):
            for b in range(vectors):
                tile = product_ref[
                    lax.rem(block, 2), s * lags : (s + 1) * lags, b * steps : (b + 1) * steps
                ]
                rows_ref[pl.ds((block * group + s) * vectors + b, 1), :] = jnp.sum(
                    skewed(tile), axis=0, keepdims=True
                )

    multiply(0)

    def body(block, carry):
        shear(block - 1)
        multiply(block)
        return carry

    lax.fori_loop(1, blocks, body, 0)
    shear(blocks - 1)
    out_ref[...] = rows_ref[...].T


def forward_of(kernels, parts, before, lags, vectors):
    rows, columns = before.shape
    width = sum(kernel.shape[1] for kernel in kernels)
    steps = columns // vectors
    sensors = rows // lags
    group = 8
    operands = [resident(value) for value in (*parts, *kernels, before)]
    return pl.pallas_call(
        functools.partial(
            forward_kernel, parts=len(parts), group=group, vectors=vectors, lags=lags, steps=steps
        ),
        out_shape=pltpu.VMEM((steps, sensors * vectors), jnp.float32),
        in_specs=[VMEM] * len(operands),
        out_specs=VMEM,
        scratch_shapes=[
            pltpu.VMEM((width, columns), jnp.bfloat16),
            pltpu.VMEM((width, columns), jnp.bfloat16),
            pltpu.VMEM((2, group * lags, columns), jnp.float32),
            pltpu.VMEM((sensors * vectors, steps), jnp.float32),
        ],
        compiler_params=room(12),
        name="forward",
    )(*operands)


def smooth_kernel(own_ref, up_ref, down_ref, taps_ref, out_ref, *, vectors, steps):
    taps, rows = taps_ref.shape
    half = (taps - 1) // 2
    weights = taps_ref[...].T
    turn = mirror(steps)
    lane = lax.broadcasted_iota(jnp.int32, (rows, steps), 1)
    for b in range(vectors):
        here = (slice(None), slice(b * steps, (b + 1) * steps))
        block = jnp.dot(
            own_ref[here] + up_ref[here] + down_ref[here], turn, precision=lax.Precision.HIGHEST
        )
        total = weights[:, half : half + 1] * block
        for k in range(taps):
            move = k - half
            if move == 0:
                continue
            moved = pltpu.roll(block, (-move) % steps, 1)
            inside = lane < steps - move if move > 0 else lane >= -move
            total = total + weights[:, k : k + 1] * jnp.where(inside, moved, 0.0)
        out_ref[:, b * steps : (b + 1) * steps] = total


def smooth_of(addends, taps, vectors):
    columns = addends[0].shape[1]
    return pl.pallas_call(
        functools.partial(smooth_kernel, vectors=vectors, steps=columns // vectors),
        out_shape=pltpu.VMEM(addends[0].shape, jnp.float32),
        in_specs=[VMEM] * 4,
        out_specs=VMEM,
        compiler_params=room(4),
        name="smooth",
    )(*(resident(value) for value in (*addends, taps)))


def send_z(value, step):
    return lax.ppermute(value, "z", ring(lax.axis_size("z"), step))


def reduce_over_z(addend_of):
    far = lax.axis_size("z") // 2
    value = addend_of(far)
    cut = value.shape[0] // 2
    up = send_z(value[:cut], 1)
    down = send_z(value[cut:], -1)
    above, below = addend_of(far - 1), addend_of(1 - far)
    up = jnp.concatenate([above[:cut] + up, above[cut:]])
    down = jnp.concatenate([below[:cut], below[cut:] + down])
    for offset in range(far - 2, -1, -1):
        up = send_z(up, 1)
        down = send_z(down, -1)
        if offset:
            up = up + addend_of(offset)
            down = down + addend_of(-offset)
    return addend_of(0), up, down


def gather_over_z(own):
    far = lax.axis_size("z") // 2
    cut = own.shape[0] // 2
    up, down = own, own
    parts = {0: own}
    for step in range(1, far):
        up = send_z(up, 1)
        down = send_z(down, -1)
        parts[-step], parts[step] = up, down
    up = send_z(up[:cut], 1)
    down = send_z(down[cut:], -1)
    parts[far] = jnp.concatenate([up, down])
    return parts


def gather_over_y(series):
    both = jnp.stack([series, swap(series, "yl")])
    yh = lax.axis_index("yh")
    other = lax.ppermute(both, ("yl", "yh"), [(i, 3 - i) for i in range(4)])[::-1]
    return jnp.stack([jnp.where(yh == 0, both, other), jnp.where(yh == 0, other, both)])


def gather_over_x(pieces):
    c, x = lax.axis_index("c"), lax.axis_index("x")
    other = swap(pieces, "c")
    here = jnp.stack([jnp.where(c == 0, pieces, other), jnp.where(c == 0, other, pieces)], 2)
    here = jnp.swapaxes(here, 0, 1)
    size = lax.axis_size("x")
    other = lax.ppermute(here, "x", [(i, i ^ 1) for i in range(size)])
    low = lax.rem(x, 2) == 0
    pair = jnp.stack([jnp.where(low, here, other), jnp.where(low, other, here)], 1)
    other = lax.ppermute(pair, "x", [(i, size - 1 - i) for i in range(size)])
    low = x < 2
    whole = jnp.stack([jnp.where(low, pair, other), jnp.where(low, other, pair)], 1)
    return whole.reshape(whole.shape[0], -1, whole.shape[-1])


def reduce_over_unk(result):
    size = lax.axis_size(UNK)
    pieces = result.reshape(size, result.shape[0] // size, result.shape[1])
    return jnp.sum(lax.all_to_all(pieces, UNK, 0, 0, tiled=True), axis=0)


def action(signals, kernel, tap_weights):
    sensors, vectors, steps_here = signals.shape
    lags, unknowns = kernel.shape[1:]
    yl, z = lax.axis_index("yl"), lax.axis_index("z")
    z_size = lax.axis_size("z")
    slot = unknowns // (2 * z_size)
    matrix = kernel.reshape(sensors * lags, unknowns)

    sent = pairs_of(matrix, 1 - yl, z, len(PAIRS))
    pieces = gather_over_y(signals.reshape(sensors * vectors, steps_here).T)
    pieces, sent = lax.optimization_barrier((pieces, sent))
    given = []
    for block in sent:
        given.append(swap(block, "yl"))
    kept = pairs_of(matrix, yl, z, 2)
    series = gather_over_x(pieces)
    own_window = window_of(series[0], lags, vectors)
    other_window = window_of(series[1], lags, vectors)
    taps = lax.dynamic_slice_in_dim(tap_weights, (yl * z_size + z) * slot, slot, 1)

    addends = {}
    for i, pair in enumerate(PAIRS):
        total = adjoint_of(
            kept[i // 2], i % 2 * 2 * slot, given[i], own_window, other_window
        )
        for j, k in enumerate(pair):
            addends[k] = total[j * slot : (j + 1) * slot]
    addends = smooth_of(reduce_over_z(lambda k: addends[k % z_size]), taps, vectors)
    smoothed = gather_over_z(addends)

    def parts_of(pairs):
        return [smoothed[k if k <= z_size // 2 else k - z_size] for pair in pairs for k in pair]

    parts = parts_of(PAIRS[2:])
    other = early_of(given[2:], parts)
    own = early_of(kept[1:], parts)
    parts = parts_of(PAIRS[:2])
    other = forward_of(given[:2], parts, other, lags, vectors)
    own = forward_of(kept[:1], parts, own, lags, vectors)
    result = reduce_over_unk(own + swap(other, "yl"))
    return result.T.reshape(sensors, vectors, steps_here)


def solution(mesh):
    sens, unk = mesh.devices.shape
    fine = Mesh(mesh.devices.reshape(sens // 2, 2, unk // 4, 2, 2), ("z", "yl", *UNK))
    sensor_axes = ("z", "yl")
    return jax.shard_map(
        action,
        mesh=fine,
        in_specs=(P(sensor_axes, None, UNK), P(sensor_axes, None, UNK), P(None, UNK)),
        out_specs=P(sensor_axes, None, UNK),
        check_vma=False,
    )
```

profile of v0, /device:TPU:1, one launch (start us, length us, event | category | flops | bytes accessed | tf_op | source)
XLA Modules:
  0.0 136.0 jit_solution(2303905424799446181)
XLA Ops:
  4.8 3.0 %collective-permute-start.1 = (f32[2,16,128]{2,1,0:T(8,128)S(1)}, f32[2,16,128]{2,1,0:T(8,128)S(1)}, u32[]{:S(2)}, u32[]{:S(2)}) collective-permute-start(f32[2,16,128]{2,1,0:T(8,128)S(1)} %pad_maximum_fusion.5), channel_id=1, source_target_pairs={{0,18},{2,16},{16,2},{18,0},{1,19},{3,17},{17,3},{19,1},{4,22},{6,... | collective-permute-start | bytes 49160 | tf_op jit(solution)/shard_map/ppermute | solution.py:360
  7.8 4.0 %pairs.3 = (f32[1024,128]{1,0:T(8,128)}, f32[1024,128]{1,0:T(8,128)S(1)}, f32[1024,128]{1,0:T(8,128)S(1)}, f32[1024,128]{1,0:T(8,128)S(1)}) custom-call(s32[2]{0:T(128)S(1)} %get-tuple-element.56.scalars_ref, f32[1024,1024]{1,0:T(8,128)} %bitcast.47), custom_call_target="tpu_custom_call" | custom-call | tf_op jit(solution)/shard_map/pairs/pallas_call | solution.py:132
  19.6 2.5 %collective-permute-start.5 = (f32[2,2,2,2,16,128]{5,4,3,2,1,0:T(8,128)}, f32[2,2,2,2,16,128]{5,4,3,2,1,0:T(8,128)S(1)}, u32[]{:S(2)}, u32[]{:S(2)}) collective-permute-start(f32[2,2,2,2,16,128]{5,4,3,2,1,0:T(8,128)} %copy.23), channel_id=1, source_target_pairs={{0,12},{4,8},{8,4},{12,0},{1,13},{5,9},{9,5},{13,1},{2,14},{6,10},... | collective-permute-start | bytes 393224 | tf_op jit(solution)/shard_map/ppermute | solution.py:373
  22.1 3.2 %pairs.2 = (f32[1024,256]{1,0:T(8,128)S(1)}, f32[1024,256]{1,0:T(8,128)S(1)}) custom-call(s32[2]{0:T(128)S(1)} %get-tuple-element.55.scalars_ref, f32[1024,1024]{1,0:T(8,128)} %bitcast.48), custom_call_target="tpu_custom_call" | custom-call | tf_op jit(solution)/shard_map/pairs/pallas_call | solution.py:132
  30.1 2.5 %adjoint.4 = f32[128,1024]{1,0:T(8,128)S(1)} custom-call(f32[1024,256]{1,0:T(8,128)S(1)} %get-tuple-element.20.kept_ref.refs_4_, f32[1024,128]{1,0:T(8,128)S(1)} %collective-permute-done.2.given_ref.refs_4_, bf16[1024,1024]{1,0:T(8,128)(2,1)S(1)} %get-tuple-element.27.kept_high_ref, bf16[1024,1024]{1,0:T(8,128)(2,1)S(1)} %get-tuple-element.28.kept_low_ref, ...), custom_call_target="tpu_custom_call" | custom-call | tf_op jit(solution)/shard_map/adjoint/pallas_call | solution.py:180
  32.7 5.7 %collective-permute-start.13 = (f32[32,1024]{1,0:T(8,128)S(1)}, f32[32,1024]{1,0:T(8,128)S(1)}, u32[]{:S(2)}, u32[]{:S(2)}) collective-permute-start(f32[32,1024]{1,0:T(8,128)S(1)} %get-tuple-element.43), channel_id=1, source_target_pairs={{0,224},{32,0},{64,32},{96,64},{128,96},{160,128},{192,160},{224,1... | collective-permute-start | bytes 393224 | tf_op jit(solution)/shard_map/ppermute | solution.py:321
  41.3 2.5 %adjoint.5 = f32[128,1024]{1,0:T(8,128)S(1)} custom-call(f32[1024,256]{1,0:T(8,128)S(1)} %get-tuple-element.20.kept_ref.refs_4_, f32[1024,128]{1,0:T(8,128)S(1)} %collective-permute-done.6.given_ref.refs_5_, bf16[1024,1024]{1,0:T(8,128)(2,1)S(1)} %get-tuple-element.27.kept_high_ref, bf16[1024,1024]{1,0:T(8,128)(2,1)S(1)} %get-tuple-element.28.kept_low_ref, ...), custom_call_target="tpu_custom_call" | custom-call | tf_op jit(solution)/shard_map/adjoint/pallas_call | solution.py:180
  44.0 5.7 %collective-permute-start.14 = (f32[64,1024]{1,0:T(8,128)S(1)}, f32[64,1024]{1,0:T(8,128)S(1)}, u32[]{:S(2)}, u32[]{:S(2)}) collective-permute-start(f32[64,1024]{1,0:T(8,128)S(1)} %pad_maximum_fusion.1), channel_id=1, source_target_pairs={{0,224},{32,0},{64,32},{96,64},{128,96},{160,128},{192,160},{224,1... | collective-permute-start | bytes 786440 | tf_op jit(solution)/shard_map/ppermute | solution.py:321
  51.7 2.5 %adjoint.6 = f32[128,1024]{1,0:T(8,128)S(1)} custom-call(f32[1024,256]{1,0:T(8,128)S(1)} %get-tuple-element.32.kept_ref.refs_4_, f32[1024,128]{1,0:T(8,128)S(1)} %collective-permute-done.9.given_ref.refs_4_, bf16[1024,1024]{1,0:T(8,128)(2,1)S(1)} %get-tuple-element.27.kept_high_ref, bf16[1024,1024]{1,0:T(8,128)(2,1)S(1)} %get-tuple-element.28.kept_low_ref, ...), custom_call_target="tpu_custom_call" | custom-call | tf_op jit(solution)/shard_map/adjoint/pallas_call | solution.py:180
  56.2 4.6 %collective-permute-start.15 = (f32[64,1024]{1,0:T(8,128)S(1)}, f32[64,1024]{1,0:T(8,128)S(1)}, u32[]{:S(2)}, u32[]{:S(2)}) collective-permute-start(f32[64,1024]{1,0:T(8,128)S(1)} %get-tuple-element.37), channel_id=1, source_target_pairs={{0,224},{32,0},{64,32},{96,64},{128,96},{160,128},{192,160},{224,1... | collective-permute-start | bytes 786440 | tf_op jit(solution)/shard_map/ppermute | solution.py:321
  62.7 2.5 %adjoint.7 = f32[128,1024]{1,0:T(8,128)S(1)} custom-call(f32[1024,256]{1,0:T(8,128)S(1)} %get-tuple-element.32.kept_ref.refs_4_, f32[1024,128]{1,0:T(8,128)S(1)} %collective-permute-done.11.given_ref.refs_5_, bf16[1024,1024]{1,0:T(8,128)(2,1)S(1)} %get-tuple-element.27.kept_high_ref, bf16[1024,1024]{1,0:T(8,128)(2,1)S(1)} %get-tuple-element.28.kept_low_ref, ...), custom_call_target="tpu_custom_call" | custom-call | tf_op jit(solution)/shard_map/adjoint/pallas_call | solution.py:180
  68.9 3.9 %collective-permute-start.16 = (f32[64,1024]{1,0:T(8,128)}, f32[64,1024]{1,0:T(8,128)}, u32[]{:S(2)}, u32[]{:S(2)}) collective-permute-start(f32[64,1024]{1,0:T(8,128)} %get-tuple-element.35), channel_id=1, source_target_pairs={{0,224},{32,0},{64,32},{96,64},{128,96},{160,128},{192,160},{224,1... | collective-permute-start | bytes 786440 | tf_op jit(solution)/shard_map/ppermute | solution.py:321
  73.9 3.4 %collective-permute-done.12.up_ref = f32[64,1024]{1,0:T(8,128)S(1)} collective-permute-done((f32[64,1024]{1,0:T(8,128)}, f32[64,1024]{1,0:T(8,128)S(1)}, u32[]{:S(2)}, u32[]{:S(2)}) %collective-permute-start.12) | collective-permute-done | bytes 262176 | tf_op jit(solution)/shard_map/ppermute | solution.py:321
  77.4 2.6 %smooth.1.refs_1_ = f32[64,1024]{1,0:T(8,128)S(1)} custom-call(f32[64,1024]{1,0:T(8,128)S(1)} %slice.73.own_ref, f32[64,1024]{1,0:T(8,128)S(1)} %collective-permute-done.12.up_ref, f32[64,1024]{1,0:T(8,128)} %collective-permute-done.16.down_ref, f32[17,64]{1,0:T(8,128)S(1)} %constant_dynamic-slice_fusion.taps_ref), custom_call_target="tpu_custom_call" | custom-call | tf_op jit(solution)/shard_map/smooth/pallas_call | solution.py:310
  80.0 2.7 %collective-permute-start.21 = (f32[64,1024]{1,0:T(8,128)S(1)}, f32[64,1024]{1,0:T(8,128)S(1)}, u32[]{:S(2)}, u32[]{:S(2)}) collective-permute-start(f32[64,1024]{1,0:T(8,128)S(1)} %smooth.1.refs_1_), channel_id=1, source_target_pairs={{0,224},{32,0},{64,32},{96,64},{128,96},{160,128},{192,160},{224,1... | collective-permute-start | bytes 786440 | tf_op jit(solution)/shard_map/ppermute | solution.py:321
  82.7 3.8 %collective-permute-done.17.refs_3_ = f32[64,1024]{1,0:T(8,128)S(1)} collective-permute-done((f32[64,1024]{1,0:T(8,128)S(1)}, f32[64,1024]{1,0:T(8,128)S(1)}, u32[]{:S(2)}, u32[]{:S(2)}) %collective-permute-start.17) | collective-permute-done | bytes 262176 | tf_op jit(solution)/shard_map/ppermute | solution.py:321
  86.6 2.5 %collective-permute-start.22 = (f32[64,1024]{1,0:T(8,128)S(1)}, f32[64,1024]{1,0:T(8,128)S(1)}, u32[]{:S(2)}, u32[]{:S(2)}) collective-permute-start(f32[64,1024]{1,0:T(8,128)S(1)} %collective-permute-done.21.refs_2_), channel_id=1, source_target_pairs={{0,224},{32,0},{64,32},{96,64},{128,96},{160,128},{192,160},{224,1... | collective-permute-start | bytes 786440 | tf_op jit(solution)/shard_map/ppermute | solution.py:321
  89.1 3.8 %collective-permute-done.18.refs_1_ = f32[64,1024]{1,0:T(8,128)S(1)} collective-permute-done((f32[64,1024]{1,0:T(8,128)S(1)}, f32[64,1024]{1,0:T(8,128)S(1)}, u32[]{:S(2)}, u32[]{:S(2)}) %collective-permute-start.18) | collective-permute-done | bytes 262176 | tf_op jit(solution)/shard_map/ppermute | solution.py:321
  92.9 2.7 %collective-permute-start.23 = (f32[64,1024]{1,0:T(8,128)S(1)}, f32[64,1024]{1,0:T(8,128)S(1)}, u32[]{:S(2)}, u32[]{:S(2)}) collective-permute-start(f32[64,1024]{1,0:T(8,128)S(1)} %collective-permute-done.22.refs_0_), channel_id=1, source_target_pairs={{0,224},{32,0},{64,32},{96,64},{128,96},{160,128},{192,160},{224,1... | collective-permute-start | bytes 786440 | tf_op jit(solution)/shard_map/ppermute | solution.py:321
  95.6 4.6 %collective-permute-done.19.refs_3_ = f32[64,1024]{1,0:T(8,128)S(1)} collective-permute-done((f32[64,1024]{1,0:T(8,128)S(1)}, f32[64,1024]{1,0:T(8,128)S(1)}, u32[]{:S(2)}, u32[]{:S(2)}) %collective-permute-start.19) | collective-permute-done | bytes 262176 | tf_op jit(solution)/shard_map/ppermute | solution.py:321
  100.3 2.9 %collective-permute-start.24 = (f32[32,1024]{1,0:T(8,128)S(1)}, f32[32,1024]{1,0:T(8,128)S(1)}, u32[]{:S(2)}, u32[]{:S(2)}) collective-permute-start(f32[32,1024]{1,0:T(8,128)S(1)} %slice.85), channel_id=1, source_target_pairs={{0,224},{32,0},{64,32},{96,64},{128,96},{160,128},{192,160},{224,1... | collective-permute-start | bytes 393224 | tf_op jit(solution)/shard_map/ppermute | solution.py:321
  107.1 2.7 %forward.3 = f32[256,128]{1,0:T(8,128)S(1)} custom-call(f32[64,1024]{1,0:T(8,128)S(1)} %constant_dynamic-update-slice_fusion.refs_0_, f32[64,1024]{1,0:T(8,128)S(1)} %smooth.1.refs_1_, f32[64,1024]{1,0:T(8,128)S(1)} %collective-permute-done.23.refs_2_, f32[64,1024]{1,0:T(8,128)S(1)} %collective-permute-done.19.refs_3_, ...), custom_call_target="tpu_custom_call" | custom-call | tf_op jit(solution)/shard_map/forward/pallas_call | solution.py:268
  112.7 2.7 %forward.2 = f32[256,128]{1,0:T(8,128)S(1)} custom-call(f32[64,1024]{1,0:T(8,128)S(1)} %constant_dynamic-update-slice_fusion.refs_0_, f32[64,1024]{1,0:T(8,128)S(1)} %smooth.1.refs_1_, f32[64,1024]{1,0:T(8,128)S(1)} %collective-permute-done.23.refs_2_, f32[64,1024]{1,0:T(8,128)S(1)} %collective-permute-done.19.refs_3_, ...), custom_call_target="tpu_custom_call" | custom-call | tf_op jit(solution)/shard_map/forward/pallas_call | solution.py:268
  115.5 19.7 %all_to_all.5 = f32[16,16,128]{2,1,0:T(8,128)S(1)} all-to-all(f32[16,16,128]{2,1,0:T(8,128)S(1)} %bitcast.49), channel_id=1, replica_groups=mesh['z'=8,'yl'=2,'x'=4,'yh'=2,'c'=2] {'x','yh','c'}, dimensions={0} | all-to-all | bytes 262144 | tf_op jit(solution)/shard_map/all_to_all | solution.py:382
  (94 shorter events, 39.0 us)
Async XLA Ops:
  0.9 3.9 %collective-permute-start = (f32[16,128]{0,1:T(8,128)S(1)}, f32[16,128]{0,1:T(8,128)S(1)}, u32[]{:S(2)}, u32[]{:S(2)}) collective-permute-start(f32[16,128]{0,1:T(8,128)S(1)} %bitcast.50), channel_id=1, source_target_pairs={{0,16},{16,0},{1,17},{17,1},{2,18},{18,2},{3,19},{19,3},{4,20},{20... | collective-permute-start | bytes 24584 | tf_op jit(solution)/shard_map/ppermute | solution.py:20
  4.8 7.8 %collective-permute-start.1 = (f32[2,16,128]{2,1,0:T(8,128)S(1)}, f32[2,16,128]{2,1,0:T(8,128)S(1)}, u32[]{:S(2)}, u32[]{:S(2)}) collective-permute-start(f32[2,16,128]{2,1,0:T(8,128)S(1)} %pad_maximum_fusion.5), channel_id=1, source_target_pairs={{0,18},{2,16},{16,2},{18,0},{1,19},{3,17},{17,3},{19,1},{4,22},{6,... | collective-permute-start | bytes 49160 | tf_op jit(solution)/shard_map/ppermute | solution.py:360
  17.0 13.1 %collective-permute-start.2 = (f32[1024,128]{1,0:T(8,128)}, f32[1024,128]{1,0:T(8,128)S(1)}, u32[]{:S(2)}, u32[]{:S(2)}) collective-permute-start(f32[1024,128]{1,0:T(8,128)} %get-tuple-element.25), channel_id=1, source_target_pairs={{0,16},{16,0},{1,17},{17,1},{2,18},{18,2},{3,19},{19,3},{4,20},{20... | collective-permute-start | bytes 1572872 | tf_op jit(solution)/shard_map/ppermute | solution.py:20
  19.6 5.8 %collective-permute-start.5 = (f32[2,2,2,2,16,128]{5,4,3,2,1,0:T(8,128)}, f32[2,2,2,2,16,128]{5,4,3,2,1,0:T(8,128)S(1)}, u32[]{:S(2)}, u32[]{:S(2)}) collective-permute-start(f32[2,2,2,2,16,128]{5,4,3,2,1,0:T(8,128)} %copy.23), channel_id=1, source_target_pairs={{0,12},{4,8},{8,4},{12,0},{1,13},{5,9},{9,5},{13,1},{2,14},{6,10},... | collective-permute-start | bytes 393224 | tf_op jit(solution)/shard_map/ppermute | solution.py:373
  25.4 16.0 %collective-permute-start.6 = (f32[1024,128]{1,0:T(8,128)}, f32[1024,128]{1,0:T(8,128)S(1)}, u32[]{:S(2)}, u32[]{:S(2)}) collective-permute-start(f32[1024,128]{1,0:T(8,128)} %copy-done.10), channel_id=1, source_target_pairs={{0,16},{16,0},{1,17},{17,1},{2,18},{18,2},{3,19},{19,3},{4,20},{20... | collective-permute-start | bytes 1572872 | tf_op jit(solution)/shard_map/ppermute | solution.py:20
  32.7 11.2 %collective-permute-start.13 = (f32[32,1024]{1,0:T(8,128)S(1)}, f32[32,1024]{1,0:T(8,128)S(1)}, u32[]{:S(2)}, u32[]{:S(2)}) collective-permute-start(f32[32,1024]{1,0:T(8,128)S(1)} %get-tuple-element.43), channel_id=1, source_target_pairs={{0,224},{32,0},{64,32},{96,64},{128,96},{160,128},{192,160},{224,1... | collective-permute-start | bytes 393224 | tf_op jit(solution)/shard_map/ppermute | solution.py:321
  38.3 5.6 %collective-permute-start.7 = (f32[32,1024]{1,0:T(8,128)S(1)}, f32[32,1024]{1,0:T(8,128)S(1)}, u32[]{:S(2)}, u32[]{:S(2)}) collective-permute-start(f32[32,1024]{1,0:T(8,128)S(1)} %get-tuple-element.44), channel_id=1, source_target_pairs={{0,32},{32,64},{64,96},{96,128},{128,160},{160,192},{192,224},{224... | collective-permute-start | bytes 393224 | tf_op jit(solution)/shard_map/ppermute | solution.py:321
  38.3 13.4 %collective-permute-start.9 = (f32[1024,128]{1,0:T(8,128)S(1)}, f32[1024,128]{1,0:T(8,128)S(1)}, u32[]{:S(2)}, u32[]{:S(2)}) collective-permute-start(f32[1024,128]{1,0:T(8,128)S(1)} %copy-done.9), channel_id=1, source_target_pairs={{0,16},{16,0},{1,17},{17,1},{2,18},{18,2},{3,19},{19,3},{4,20},{20... | collective-permute-start | bytes 1572872 | tf_op jit(solution)/shard_map/ppermute | solution.py:20
  44.0 10.3 %collective-permute-start.14 = (f32[64,1024]{1,0:T(8,128)S(1)}, f32[64,1024]{1,0:T(8,128)S(1)}, u32[]{:S(2)}, u32[]{:S(2)}) collective-permute-start(f32[64,1024]{1,0:T(8,128)S(1)} %pad_maximum_fusion.1), channel_id=1, source_target_pairs={{0,224},{32,0},{64,32},{96,64},{128,96},{160,128},{192,160},{224,1... | collective-permute-start | bytes 786440 | tf_op jit(solution)/shard_map/ppermute | solution.py:321
  49.6 6.5 %collective-permute-start.8 = (f32[64,1024]{1,0:T(8,128)S(1)}, f32[64,1024]{1,0:T(8,128)S(1)}, u32[]{:S(2)}, u32[]{:S(2)}) collective-permute-start(f32[64,1024]{1,0:T(8,128)S(1)} %pad_maximum_fusion), channel_id=1, source_target_pairs={{0,32},{32,64},{64,96},{96,128},{128,160},{160,192},{192,224},{224... | collective-permute-start | bytes 786440 | tf_op jit(solution)/shard_map/ppermute | solution.py:321
  49.7 12.9 %collective-permute-start.11 = (f32[1024,128]{1,0:T(8,128)S(1)}, f32[1024,128]{1,0:T(8,128)S(1)}, u32[]{:S(2)}, u32[]{:S(2)}) collective-permute-start(f32[1024,128]{1,0:T(8,128)S(1)} %copy-done.7), channel_id=1, source_target_pairs={{0,16},{16,0},{1,17},{17,1},{2,18},{18,2},{3,19},{19,3},{4,20},{20... | collective-permute-start | bytes 1572872 | tf_op jit(solution)/shard_map/ppermute | solution.py:20
  56.2 9.0 %collective-permute-start.15 = (f32[64,1024]{1,0:T(8,128)S(1)}, f32[64,1024]{1,0:T(8,128)S(1)}, u32[]{:S(2)}, u32[]{:S(2)}) collective-permute-start(f32[64,1024]{1,0:T(8,128)S(1)} %get-tuple-element.37), channel_id=1, source_target_pairs={{0,224},{32,0},{64,32},{96,64},{128,96},{160,128},{192,160},{224,1... | collective-permute-start | bytes 786440 | tf_op jit(solution)/shard_map/ppermute | solution.py:321
  60.8 6.4 %collective-permute-start.10 = (f32[64,1024]{1,0:T(8,128)S(1)}, f32[64,1024]{1,0:T(8,128)S(1)}, u32[]{:S(2)}, u32[]{:S(2)}) collective-permute-start(f32[64,1024]{1,0:T(8,128)S(1)} %get-tuple-element.38), channel_id=1, source_target_pairs={{0,32},{32,64},{64,96},{96,128},{128,160},{160,192},{192,224},{224... | collective-permute-start | bytes 786440 | tf_op jit(solution)/shard_map/ppermute | solution.py:321
  68.2 9.2 %collective-permute-start.12 = (f32[64,1024]{1,0:T(8,128)}, f32[64,1024]{1,0:T(8,128)S(1)}, u32[]{:S(2)}, u32[]{:S(2)}) collective-permute-start(f32[64,1024]{1,0:T(8,128)} %get-tuple-element.36), channel_id=1, source_target_pairs={{0,32},{32,64},{64,96},{96,128},{128,160},{160,192},{192,224},{224... | collective-permute-start | bytes 786440 | tf_op jit(solution)/shard_map/ppermute | solution.py:321
  68.9 8.5 %collective-permute-start.16 = (f32[64,1024]{1,0:T(8,128)}, f32[64,1024]{1,0:T(8,128)}, u32[]{:S(2)}, u32[]{:S(2)}) collective-permute-start(f32[64,1024]{1,0:T(8,128)} %get-tuple-element.35), channel_id=1, source_target_pairs={{0,224},{32,0},{64,32},{96,64},{128,96},{160,128},{192,160},{224,1... | collective-permute-start | bytes 786440 | tf_op jit(solution)/shard_map/ppermute | solution.py:321
  79.9 6.5 %collective-permute-start.17 = (f32[64,1024]{1,0:T(8,128)S(1)}, f32[64,1024]{1,0:T(8,128)S(1)}, u32[]{:S(2)}, u32[]{:S(2)}) collective-permute-start(f32[64,1024]{1,0:T(8,128)S(1)} %smooth.1.refs_1_), channel_id=1, source_target_pairs={{0,32},{32,64},{64,96},{96,128},{128,160},{160,192},{192,224},{224... | collective-permute-start | bytes 786440 | tf_op jit(solution)/shard_map/ppermute | solution.py:321
  80.0 6.6 %collective-permute-start.21 = (f32[64,1024]{1,0:T(8,128)S(1)}, f32[64,1024]{1,0:T(8,128)S(1)}, u32[]{:S(2)}, u32[]{:S(2)}) collective-permute-start(f32[64,1024]{1,0:T(8,128)S(1)} %smooth.1.refs_1_), channel_id=1, source_target_pairs={{0,224},{32,0},{64,32},{96,64},{128,96},{160,128},{192,160},{224,1... | collective-permute-start | bytes 786440 | tf_op jit(solution)/shard_map/ppermute | solution.py:321
  86.5 6.4 %collective-permute-start.18 = (f32[64,1024]{1,0:T(8,128)S(1)}, f32[64,1024]{1,0:T(8,128)S(1)}, u32[]{:S(2)}, u32[]{:S(2)}) collective-permute-start(f32[64,1024]{1,0:T(8,128)S(1)} %collective-permute-done.17.refs_3_), channel_id=1, source_target_pairs={{0,32},{32,64},{64,96},{96,128},{128,160},{160,192},{192,224},{224... | collective-permute-start | bytes 786440 | tf_op jit(solution)/shard_map/ppermute | solution.py:321
  86.6 6.3 %collective-permute-start.22 = (f32[64,1024]{1,0:T(8,128)S(1)}, f32[64,1024]{1,0:T(8,128)S(1)}, u32[]{:S(2)}, u32[]{:S(2)}) collective-permute-start(f32[64,1024]{1,0:T(8,128)S(1)} %collective-permute-done.21.refs_2_), channel_id=1, source_target_pairs={{0,224},{32,0},{64,32},{96,64},{128,96},{160,128},{192,160},{224,1... | collective-permute-start | bytes 786440 | tf_op jit(solution)/shard_map/ppermute | solution.py:321
  92.9 7.3 %collective-permute-start.19 = (f32[64,1024]{1,0:T(8,128)S(1)}, f32[64,1024]{1,0:T(8,128)S(1)}, u32[]{:S(2)}, u32[]{:S(2)}) collective-permute-start(f32[64,1024]{1,0:T(8,128)S(1)} %collective-permute-done.18.refs_1_), channel_id=1, source_target_pairs={{0,32},{32,64},{64,96},{96,128},{128,160},{160,192},{192,224},{224... | collective-permute-start | bytes 786440 | tf_op jit(solution)/shard_map/ppermute | solution.py:321
  92.9 7.4 %collective-permute-start.23 = (f32[64,1024]{1,0:T(8,128)S(1)}, f32[64,1024]{1,0:T(8,128)S(1)}, u32[]{:S(2)}, u32[]{:S(2)}) collective-permute-start(f32[64,1024]{1,0:T(8,128)S(1)} %collective-permute-done.22.refs_0_), channel_id=1, source_target_pairs={{0,224},{32,0},{64,32},{96,64},{128,96},{160,128},{192,160},{224,1... | collective-permute-start | bytes 786440 | tf_op jit(solution)/shard_map/ppermute | solution.py:321
  100.2 6.8 %collective-permute-start.20 = (f32[32,1024]{1,0:T(8,128)S(1)}, f32[32,1024]{1,0:T(8,128)S(1)}, u32[]{:S(2)}, u32[]{:S(2)}) collective-permute-start(f32[32,1024]{1,0:T(8,128)S(1)} %slice.84), channel_id=1, source_target_pairs={{0,32},{32,64},{64,96},{96,128},{128,160},{160,192},{192,224},{224... | collective-permute-start | bytes 393224 | tf_op jit(solution)/shard_map/ppermute | solution.py:321
  100.3 6.7 %collective-permute-start.24 = (f32[32,1024]{1,0:T(8,128)S(1)}, f32[32,1024]{1,0:T(8,128)S(1)}, u32[]{:S(2)}, u32[]{:S(2)}) collective-permute-start(f32[32,1024]{1,0:T(8,128)S(1)} %slice.85), channel_id=1, source_target_pairs={{0,224},{32,0},{64,32},{96,64},{128,96},{160,128},{192,160},{224,1... | collective-permute-start | bytes 393224 | tf_op jit(solution)/shard_map/ppermute | solution.py:321
  109.8 5.6 %collective-permute-start.25 = (f32[256,128]{1,0:T(8,128)S(1)}, f32[256,128]{1,0:T(8,128)S(1)}, u32[]{:S(2)}, u32[]{:S(2)}) collective-permute-start(f32[256,128]{1,0:T(8,128)S(1)} %forward.3), channel_id=1, source_target_pairs={{0,16},{16,0},{1,17},{17,1},{2,18},{18,2},{3,19},{19,3},{4,20},{20... | collective-permute-start | bytes 393224 | tf_op jit(solution)/shard_map/ppermute | solution.py:20
  (13 other events, 190.2 us)
where the time goes:
time: 136 us
  starting transfers between devices  44.5 us (33%)
  Pallas kernels  34.2 us (25%)
  waiting for transfers between devices  31.6 us (23%)
  blocking collectives  19.7 us (14%)
  local copies, waits for them, and re-layouts  4.46 us (3%)
    ppermute x16, starting transfers between devices, send_z(): return lax.ppermute(value, 'z', ring(lax.axis_size('z'), step))  31.6 us
    ppermute x16, waiting for transfers between devices, send_z(): return lax.ppermute(value, 'z', ring(lax.axis_size('z'), step))  21 us
    all_to_all x1, blocking collectives, reduce_over_unk(): return jnp.sum(lax.all_to_all(pieces, UNK, 0, 0, tiled=True), axis=0)  19.7 us
    pallas_call x4, Pallas kernels, adjoint_of(): pl.pallas_call(functools.partial(adjoint_kernel, first=first, block=256),...  10.1 us
    ppermute x7, waiting for transfers between devices, swap(): return lax.ppermute(value, axis, [(0, 1), (1, 0)])  8.63 us
    pallas_call x2, Pallas kernels, pairs_of(): pl.pallas_call(functools.partial(pair_kernel, lanes=width // len(PAIRS)),...  7.21 us
    ppermute x7, starting transfers between devices, swap(): return lax.ppermute(value, axis, [(0, 1), (1, 0)])  6.11 us
    pallas_call x2, Pallas kernels, forward_of(): pl.pallas_call(functools.partial(forward_kernel, parts=len(parts), group=...  5.44 us
  transfers between devices with their start and end apart: 26, of which 15 were waited for; matrix products, arithmetic and copies ran while one was open for 2% of the time, Pallas kernels for 21%

commit v1 on v0

--- a/solution.py
+++ b/solution.py
@@ -83,9 +83,10 @@
     )(resident(series))
 
 
-def pair_kernel(scalars_ref, kernel_ref, *refs, lanes):
+def pair_kernel(place_ref, kernel_ref, *refs, pairs, lanes, other):
     *out_refs, half_ref, arrived = refs
-    half, z = scalars_ref[0], scalars_ref[1]
+    half, z = place_ref[0], place_ref[1]
+    half = 1 - half if other else half
     slots = 2 * len(PAIRS)
     slot = lanes // 2
     rows, width = half_ref.shape
@@ -113,10 +114,10 @@
             shift = lax.rem(lax.rem(place, 2) + high, 2) * slot
             return pltpu.roll(half_ref[here, pl.ds(start, lanes)], shift, 1)
 
-        pairs = iter(PAIRS)
+        left = iter(pairs)
         for out_ref in out_refs:
             for start in range(0, out_ref.shape[1], lanes):
-                low, high = next(pairs)
+                low, high = next(left)
                 out_ref[here, start : start + lanes] = jnp.where(
                     lane < slot, half_of(low, 0), half_of(high, 1)
                 )
@@ -125,13 +126,14 @@
     lax.fori_loop(0, blocks, body, 0)
 
 
-def pairs_of(matrix, half, z, outputs):
+def pairs_of(matrix, place, other, pairs, outputs):
     rows, unknowns = matrix.shape
     width = unknowns // 2
+    lanes = width // len(PAIRS)
     blocks = 8
     return pl.pallas_call(
-        functools.partial(pair_kernel, lanes=width // len(PAIRS)),
-        out_shape=[pltpu.VMEM((rows, width // outputs), jnp.float32)] * outputs,
+        functools.partial(pair_kernel, pairs=pairs, lanes=lanes, other=other),
+        out_shape=[pltpu.VMEM((rows, lanes * len(pairs) // outputs), jnp.float32)] * outputs,
         in_specs=[
             pl.BlockSpec(memory_space=pltpu.SMEM),
             pl.BlockSpec(memory_space=pltpu.HBM),
@@ -143,10 +145,7 @@
         ],
         compiler_params=room(4),
         name="pairs",
-    )(
-        jnp.stack([half, z]).astype(jnp.int32),
-        pltpu.with_memory_space_constraint(matrix, pltpu.HBM),
-    )
+    )(place, pltpu.with_memory_space_constraint(matrix, pltpu.HBM))
 
 
 def three_pass(high, low, right_high, right_low):
@@ -157,31 +156,35 @@
 
 
 def adjoint_kernel(
-    kept_ref, given_ref, kept_high_ref, kept_low_ref, given_high_ref, given_low_ref, out_ref,
-    *, first, block,
+    kept_ref, given_ref, kept_high_ref, kept_low_ref, given_high_ref, given_low_ref, *out_refs,
+    first, block,
 ):
-    out_ref[...] = jnp.zeros(out_ref.shape, jnp.float32)
     width = given_ref.shape[1]
+    slot = width // 2
+    for out_ref in out_refs:
+        out_ref[...] = jnp.zeros(out_ref.shape, jnp.float32)
 
     def body(i, carry):
         here = pl.ds(pl.multiple_of(i * block, block), block)
         kept = split(kept_ref[here, first : first + width].T)
         given = split(given_ref[here, :].T)
-        out_ref[...] += three_pass(
+        total = three_pass(
             *kept, kept_high_ref[here, :], kept_low_ref[here, :]
         ) + three_pass(*given, given_high_ref[here, :], given_low_ref[here, :])
+        for i, out_ref in enumerate(out_refs):
+            out_ref[...] += total[i * slot : (i + 1) * slot]
         return carry
 
     lax.fori_loop(0, given_ref.shape[0] // block, body, 0)
 
 
 def adjoint_of(kept, first, given, own_window, other_window):
-    operands = [resident(value) for value in (kept, given, *own_window, *other_window)]
+    operands = [resident(kept), given, *(resident(value) for value in (*own_window, *other_window))]
     return pl.pallas_call(
         functools.partial(adjoint_kernel, first=first, block=256),
-        out_shape=pltpu.VMEM((given.shape[1], own_window[0].shape[1]), jnp.float32),
+        out_shape=[pltpu.VMEM((given.shape[1] // 2, own_window[0].shape[1]), jnp.float32)] * 2,
         in_specs=[VMEM] * len(operands),
-        out_specs=VMEM,
+        out_specs=[VMEM] * 2,
         compiler_params=room(8),
         name="adjoint",
     )(*operands)
@@ -283,16 +286,18 @@
     )(*operands)
 
 
-def smooth_kernel(own_ref, up_ref, down_ref, taps_ref, out_ref, *, vectors, steps):
-    taps, rows = taps_ref.shape
+def smooth_kernel(place_ref, series_ref, taps_ref, out_ref, *, vectors, steps):
+    taps = taps_ref.shape[0]
+    rows = series_ref.shape[0]
     half = (taps - 1) // 2
-    weights = taps_ref[...].T
+    slot = place_ref[0] * (taps_ref.shape[1] // (2 * rows)) + place_ref[1]
+    pair = taps_ref[:, pl.ds(pl.multiple_of(slot // 2 * 2 * rows, 2 * rows), 2 * rows)]
+    weights = pltpu.roll(pair, lax.rem(slot, 2) * rows, 1).T[:rows]
     turn = mirror(steps)
     lane = lax.broadcasted_iota(jnp.int32, (rows, steps), 1)
     for b in range(vectors):
-        here = (slice(None), slice(b * steps, (b + 1) * steps))
         block = jnp.dot(
-            own_ref[here] + up_ref[here] + down_ref[here], turn, precision=lax.Precision.HIGHEST
+            series_ref[:, b * steps : (b + 1) * steps], turn, precision=lax.Precision.HIGHEST
         )
         total = weights[:, half : half + 1] * block
         for k in range(taps):
@@ -305,16 +310,16 @@
         out_ref[:, b * steps : (b + 1) * steps] = total
 
 
-def smooth_of(addends, taps, vectors):
-    columns = addends[0].shape[1]
+def smooth_of(series, taps, place, vectors):
+    columns = series.shape[1]
     return pl.pallas_call(
         functools.partial(smooth_kernel, vectors=vectors, steps=columns // vectors),
-        out_shape=pltpu.VMEM(addends[0].shape, jnp.float32),
-        in_specs=[VMEM] * 4,
+        out_shape=pltpu.VMEM(series.shape, jnp.float32),
+        in_specs=[pl.BlockSpec(memory_space=pltpu.SMEM), VMEM, VMEM],
         out_specs=VMEM,
         compiler_params=room(4),
         name="smooth",
-    )(*(resident(value) for value in (*addends, taps)))
+    )(place, resident(series), resident(taps))
 
 
 def send_z(value, step):
@@ -336,7 +341,7 @@
         if offset:
             up = up + addend_of(offset)
             down = down + addend_of(-offset)
-    return addend_of(0), up, down
+    return addend_of(0) + up + down
 
 
 def gather_over_z(own):
@@ -354,24 +359,21 @@
     return parts
 
 
-def gather_over_y(series):
-    both = jnp.stack([series, swap(series, "yl")])
-    yh = lax.axis_index("yh")
+def gather_over_y(series, low):
+    other = swap(series, "yl")
+    both = jnp.stack([series, other])
     other = lax.ppermute(both, ("yl", "yh"), [(i, 3 - i) for i in range(4)])[::-1]
-    return jnp.stack([jnp.where(yh == 0, both, other), jnp.where(yh == 0, other, both)])
-
-
-def gather_over_x(pieces):
-    c, x = lax.axis_index("c"), lax.axis_index("x")
+    return jnp.stack([jnp.where(low, both, other), jnp.where(low, other, both)])
+
+
+def gather_over_x(pieces, first, even, low):
     other = swap(pieces, "c")
-    here = jnp.stack([jnp.where(c == 0, pieces, other), jnp.where(c == 0, other, pieces)], 2)
+    here = jnp.stack([jnp.where(first, pieces, other), jnp.where(first, other, pieces)], 2)
     here = jnp.swapaxes(here, 0, 1)
     size = lax.axis_size("x")
     other = lax.ppermute(here, "x", [(i, i ^ 1) for i in range(size)])
-    low = lax.rem(x, 2) == 0
-    pair = jnp.stack([jnp.where(low, here, other), jnp.where(low, other, here)], 1)
+    pair = jnp.stack([jnp.where(even, here, other), jnp.where(even, other, here)], 1)
     other = lax.ppermute(pair, "x", [(i, size - 1 - i) for i in range(size)])
-    low = x < 2
     whole = jnp.stack([jnp.where(low, pair, other), jnp.where(low, other, pair)], 1)
     return whole.reshape(whole.shape[0], -1, whole.shape[-1])
 
@@ -385,31 +387,34 @@
 def action(signals, kernel, tap_weights):
     sensors, vectors, steps_here = signals.shape
     lags, unknowns = kernel.shape[1:]
-    yl, z = lax.axis_index("yl"), lax.axis_index("z")
     z_size = lax.axis_size("z")
+    x, yh, c = (lax.axis_index(name) for name in UNK)
+    place = jnp.stack([lax.axis_index("yl"), lax.axis_index("z")]).astype(jnp.int32)
+    signals, place, lower, *sides = lax.optimization_barrier(
+        (signals, place, yh == 0, c == 0, lax.rem(x, 2) == 0, x < 2)
+    )
     slot = unknowns // (2 * z_size)
     matrix = kernel.reshape(sensors * lags, unknowns)
 
-    sent = pairs_of(matrix, 1 - yl, z, len(PAIRS))
-    pieces = gather_over_y(signals.reshape(sensors * vectors, steps_here).T)
-    pieces, sent = lax.optimization_barrier((pieces, sent))
-    given = []
-    for block in sent:
-        given.append(swap(block, "yl"))
-    kept = pairs_of(matrix, yl, z, 2)
-    series = gather_over_x(pieces)
+    pieces = gather_over_y(signals.reshape(sensors * vectors, steps_here).T, lower)
+    given, kept = [], []
+    for i in range(2):
+        pairs = PAIRS[2 * i : 2 * i + 2]
+        sent = pairs_of(matrix, place, True, pairs, 2)
+        for block in sent:
+            given.append(swap(block, "yl"))
+        kept += pairs_of(matrix, place, False, pairs, 1)
+    series = gather_over_x(pieces, *sides)
     own_window = window_of(series[0], lags, vectors)
     other_window = window_of(series[1], lags, vectors)
-    taps = lax.dynamic_slice_in_dim(tap_weights, (yl * z_size + z) * slot, slot, 1)
-
     addends = {}
     for i, pair in enumerate(PAIRS):
-        total = adjoint_of(
+        addends[pair[0]], addends[pair[1]] = adjoint_of(
             kept[i // 2], i % 2 * 2 * slot, given[i], own_window, other_window
         )
-        for j, k in enumerate(pair):
-            addends[k] = total[j * slot : (j + 1) * slot]
-    addends = smooth_of(reduce_over_z(lambda k: addends[k % z_size]), taps, vectors)
+    addends = smooth_of(
+        reduce_over_z(lambda k: addends[k % z_size]), tap_weights, place, vectors
+    )
     smoothed = gather_over_z(addends)
 
     def parts_of(pairs):

time: 136 us -> 137 us (level)
  blocking collectives: 19.7 us -> 23.2 us
  Pallas kernels: 34.2 us -> 37.2 us
  local copies, waits for them, and re-layouts: 4.46 us -> 1.82 us
  waiting for transfers between devices: 31.6 us -> 29.8 us
    ppermute x7, starting transfers between devices: 6.11 us -> 10.3 us  [swap(): return lax.ppermute(value, axis, [(0, 1), (1, 0)])]
    pallas_call x2 -> x4, Pallas kernels: 7.21 us -> 10.8 us  [pairs_of(): pl.pallas_call(functools.partial(pair_kernel, pairs=pairs, lanes=lanes, o...]
    all_to_all x1, blocking collectives: 19.7 us -> 23.2 us  [reduce_over_unk(): return jnp.sum(lax.all_to_all(pieces, UNK, 0, 0, tiled=True), axis=0)]
    ppermute x16, starting transfers between devices: 31.6 us -> 29.7 us  [send_z(): return lax.ppermute(value, 'z', ring(lax.axis_size('z'), step))]
    unnamed x24 -> x3, local copies, waits for them, and re-layouts: 1.74 us -> 0.02 us
    ppermute x1, waiting for transfers between devices: 1.9 us -> 0.28 us  [gather_over_x(): other = lax.ppermute(here, 'x', [(i, i ^ 1) for i in range(size)])]
  transfers between devices with their start and end apart: 26 -> 26, of which waited for: 15 -> 14; matrix products, arithmetic and copies ran while one was open for 2% -> 0% of each run, Pallas kernels for 21% -> 24%
where the time goes in v1:
time: 137 us
  starting transfers between devices  44.2 us (32%)
  Pallas kernels  37.2 us (27%)
  waiting for transfers between devices  29.8 us (22%)
  blocking collectives  23.2 us (17%)
  local copies, waits for them, and re-layouts  1.82 us (1%)
    ppermute x16, starting transfers between devices, send_z(): return lax.ppermute(value, 'z', ring(lax.axis_size('z'), step))  29.7 us
    all_to_all x1, blocking collectives, reduce_over_unk(): return jnp.sum(lax.all_to_all(pieces, UNK, 0, 0, tiled=True), axis=0)  23.2 us
    ppermute x16, waiting for transfers between devices, send_z(): return lax.ppermute(value, 'z', ring(lax.axis_size('z'), step))  19.7 us
    pallas_call x4, Pallas kernels, pairs_of(): pl.pallas_call(functools.partial(pair_kernel, pairs=pairs, lanes=lanes, o...  10.8 us
    ppermute x7, starting transfers between devices, swap(): return lax.ppermute(value, axis, [(0, 1), (1, 0)])  10.3 us
    pallas_call x4, Pallas kernels, adjoint_of(): pl.pallas_call(functools.partial(adjoint_kernel, first=first, block=256),...  9.92 us
    ppermute x7, waiting for transfers between devices, swap(): return lax.ppermute(value, axis, [(0, 1), (1, 0)])  8.65 us
    pallas_call x2, Pallas kernels, forward_of(): pl.pallas_call(functools.partial(forward_kernel, parts=len(parts), group=...  5.45 us
  transfers between devices with their start and end apart: 26, of which 14 were waited for; matrix products, arithmetic and copies ran while one was open for 0% of the time, Pallas kernels for 24%

profile of v1, /device:TPU:1, one launch (start us, length us, event | category | flops | bytes accessed | tf_op | source)
XLA Modules:
  0.0 137.1 jit_solution(2357531373571140277)
XLA Ops:
  4.8 3.0 %collective-permute-start.2 = (f32[2,16,128]{2,1,0:T(8,128)S(1)}, f32[2,16,128]{2,1,0:T(8,128)S(1)}, u32[]{:S(2)}, u32[]{:S(2)}) collective-permute-start(f32[2,16,128]{2,1,0:T(8,128)S(1)} %pad_maximum_fusion.5), channel_id=1, source_target_pairs={{0,18},{2,16},{16,2},{18,0},{1,19},{3,17},{17,3},{19,1},{4,22},{6,... | collective-permute-start | bytes 49160 | tf_op jit(solution)/shard_map/ppermute | solution.py:365
  8.9 4.7 %collective-permute-start.3 = (f32[2,2,16,128]{3,2,1,0:T(8,128)S(1)}, f32[2,2,16,128]{3,2,1,0:T(8,128)S(1)}, u32[]{:S(2)}, u32[]{:S(2)}) collective-permute-start(f32[2,2,16,128]{3,2,1,0:T(8,128)S(1)} %pad_maximum_fusion.4), channel_id=1, source_target_pairs={{0,1},{1,0},{2,3},{3,2},{4,5},{5,4},{6,7},{7,6},{8,9},{9,8},{10,11... | collective-permute-start | bytes 98312 | tf_op jit(solution)/shard_map/ppermute | solution.py:20
  14.6 2.7 %pairs.5 = (f32[1024,128]{1,0:T(8,128)S(1)}, f32[1024,128]{1,0:T(8,128)S(1)}) custom-call(s32[2]{0:T(128)S(1)} %pad_add_fusion.place_ref, f32[1024,1024]{1,0:T(8,128)} %bitcast.46), custom_call_target="tpu_custom_call" | custom-call | tf_op jit(solution)/shard_map/pairs/pallas_call | solution.py:134
  20.3 2.7 %pairs.4.kept_ref.refs_4_ = f32[1024,256]{1,0:T(8,128)S(1)} custom-call(s32[2]{0:T(128)S(1)} %pad_add_fusion.place_ref, f32[1024,1024]{1,0:T(8,128)} %bitcast.47), custom_call_target="tpu_custom_call" | custom-call | tf_op jit(solution)/shard_map/pairs/pallas_call | solution.py:134
  27.1 3.4 %collective-permute-done.given_ref.refs_4_ = f32[1024,128]{1,0:T(8,128)S(1)} collective-permute-done((f32[1024,128]{1,0:T(8,128)S(1)}, f32[1024,128]{1,0:T(8,128)S(1)}, u32[]{:S(2)}, u32[]{:S(2)}) %collective-permute-start) | collective-permute-done | bytes 524320 | tf_op jit(solution)/shard_map/ppermute | solution.py:20
  33.1 4.9 %collective-permute-start.13 = (f32[32,1024]{1,0:T(8,128)S(1)}, f32[32,1024]{1,0:T(8,128)S(1)}, u32[]{:S(2)}, u32[]{:S(2)}) collective-permute-start(f32[32,1024]{1,0:T(8,128)S(1)} %get-tuple-element.52), channel_id=1, source_target_pairs={{0,224},{32,0},{64,32},{96,64},{128,96},{160,128},{192,160},{224,1... | collective-permute-start | bytes 393224 | tf_op jit(solution)/shard_map/ppermute | solution.py:326
  37.9 2.7 %pairs.7 = (f32[1024,128]{1,0:T(8,128)S(1)}, f32[1024,128]{1,0:T(8,128)S(1)}) custom-call(s32[2]{0:T(128)S(1)} %pad_add_fusion.place_ref, f32[1024,1024]{1,0:T(8,128)} %bitcast.48), custom_call_target="tpu_custom_call" | custom-call | tf_op jit(solution)/shard_map/pairs/pallas_call | solution.py:134
  42.2 2.5 %adjoint.5 = (f32[64,1024]{1,0:T(8,128)S(1)}, f32[64,1024]{1,0:T(8,128)S(1)}) custom-call(f32[1024,256]{1,0:T(8,128)S(1)} %pairs.4.kept_ref.refs_4_, f32[1024,128]{1,0:T(8,128)S(1)} %collective-permute-done.6.given_ref.refs_5_, bf16[1024,1024]{1,0:T(8,128)(2,1)S(1)} %get-tuple-element.34.kept_high_ref, ...), custom_call_target="tpu_custom_call" | custom-call | tf_op jit(solution)/shard_map/adjoint/pallas_call | solution.py:183
  45.3 4.0 %collective-permute-start.14 = (f32[64,1024]{1,0:T(8,128)S(1)}, f32[64,1024]{1,0:T(8,128)S(1)}, u32[]{:S(2)}, u32[]{:S(2)}) collective-permute-start(f32[64,1024]{1,0:T(8,128)S(1)} %pad_maximum_fusion.1), channel_id=1, source_target_pairs={{0,224},{32,0},{64,32},{96,64},{128,96},{160,128},{192,160},{224,1... | collective-permute-start | bytes 786440 | tf_op jit(solution)/shard_map/ppermute | solution.py:326
  49.4 2.7 %pairs.6.kept_ref.refs_4_ = f32[1024,256]{1,0:T(8,128)S(1)} custom-call(s32[2]{0:T(128)S(1)} %pad_add_fusion.place_ref, f32[1024,1024]{1,0:T(8,128)} %bitcast.49), custom_call_target="tpu_custom_call" | custom-call | tf_op jit(solution)/shard_map/pairs/pallas_call | solution.py:134
  52.1 2.5 %adjoint.6 = (f32[64,1024]{1,0:T(8,128)S(1)}, f32[64,1024]{1,0:T(8,128)S(1)}) custom-call(f32[1024,256]{1,0:T(8,128)S(1)} %pairs.6.kept_ref.refs_4_, f32[1024,128]{1,0:T(8,128)S(1)} %collective-permute-done.9.given_ref.refs_4_, bf16[1024,1024]{1,0:T(8,128)(2,1)S(1)} %get-tuple-element.34.kept_high_ref, ...), custom_call_target="tpu_custom_call" | custom-call | tf_op jit(solution)/shard_map/adjoint/pallas_call | solution.py:183
  56.5 3.3 %collective-permute-start.15 = (f32[64,1024]{1,0:T(8,128)S(1)}, f32[64,1024]{1,0:T(8,128)S(1)}, u32[]{:S(2)}, u32[]{:S(2)}) collective-permute-start(f32[64,1024]{1,0:T(8,128)S(1)} %add.32), channel_id=1, source_target_pairs={{0,224},{32,0},{64,32},{96,64},{128,96},{160,128},{192,160},{224,1... | collective-permute-start | bytes 786440 | tf_op jit(solution)/shard_map/ppermute | solution.py:326
  59.8 2.8 %collective-permute-done.11.given_ref.refs_5_ = f32[1024,128]{1,0:T(8,128)S(1)} collective-permute-done((f32[1024,128]{1,0:T(8,128)S(1)}, f32[1024,128]{1,0:T(8,128)S(1)}, u32[]{:S(2)}, u32[]{:S(2)}) %collective-permute-start.11) | collective-permute-done | bytes 524320 | tf_op jit(solution)/shard_map/ppermute | solution.py:20
  62.6 2.5 %adjoint.7 = (f32[64,1024]{1,0:T(8,128)S(1)}, f32[64,1024]{1,0:T(8,128)S(1)}) custom-call(f32[1024,256]{1,0:T(8,128)S(1)} %pairs.6.kept_ref.refs_4_, f32[1024,128]{1,0:T(8,128)S(1)} %collective-permute-done.11.given_ref.refs_5_, bf16[1024,1024]{1,0:T(8,128)(2,1)S(1)} %get-tuple-element.34.kept_high_ref, ...), custom_call_target="tpu_custom_call" | custom-call | tf_op jit(solution)/shard_map/adjoint/pallas_call | solution.py:183
  65.1 2.6 %collective-permute-start.12 = (f32[64,1024]{1,0:T(8,128)S(1)}, f32[64,1024]{1,0:T(8,128)S(1)}, u32[]{:S(2)}, u32[]{:S(2)}) collective-permute-start(f32[64,1024]{1,0:T(8,128)S(1)} %add.29), channel_id=1, source_target_pairs={{0,32},{32,64},{64,96},{96,128},{128,160},{160,192},{192,224},{224... | collective-permute-start | bytes 786440 | tf_op jit(solution)/shard_map/ppermute | solution.py:326
  67.8 3.1 %collective-permute-start.16 = (f32[64,1024]{1,0:T(8,128)S(1)}, f32[64,1024]{1,0:T(8,128)S(1)}, u32[]{:S(2)}, u32[]{:S(2)}) collective-permute-start(f32[64,1024]{1,0:T(8,128)S(1)} %add.33), channel_id=1, source_target_pairs={{0,224},{32,0},{64,32},{96,64},{128,96},{160,128},{192,160},{224,1... | collective-permute-start | bytes 786440 | tf_op jit(solution)/shard_map/ppermute | solution.py:326
  70.9 4.1 %collective-permute-done.12 = f32[64,1024]{1,0:T(8,128)S(1)} collective-permute-done((f32[64,1024]{1,0:T(8,128)S(1)}, f32[64,1024]{1,0:T(8,128)S(1)}, u32[]{:S(2)}, u32[]{:S(2)}) %collective-permute-start.12) | collective-permute-done | bytes 262176 | tf_op jit(solution)/shard_map/ppermute | solution.py:326
  79.9 3.8 %collective-permute-done.17.refs_3_ = f32[64,1024]{1,0:T(8,128)S(1)} collective-permute-done((f32[64,1024]{1,0:T(8,128)S(1)}, f32[64,1024]{1,0:T(8,128)S(1)}, u32[]{:S(2)}, u32[]{:S(2)}) %collective-permute-start.17) | collective-permute-done | bytes 262176 | tf_op jit(solution)/shard_map/ppermute | solution.py:326
  86.4 3.8 %collective-permute-done.18.refs_1_ = f32[64,1024]{1,0:T(8,128)S(1)} collective-permute-done((f32[64,1024]{1,0:T(8,128)S(1)}, f32[64,1024]{1,0:T(8,128)S(1)}, u32[]{:S(2)}, u32[]{:S(2)}) %collective-permute-start.18) | collective-permute-done | bytes 262176 | tf_op jit(solution)/shard_map/ppermute | solution.py:326
  93.0 5.0 %collective-permute-done.19.refs_3_ = f32[64,1024]{1,0:T(8,128)S(1)} collective-permute-done((f32[64,1024]{1,0:T(8,128)S(1)}, f32[64,1024]{1,0:T(8,128)S(1)}, u32[]{:S(2)}, u32[]{:S(2)}) %collective-permute-start.19) | collective-permute-done | bytes 262176 | tf_op jit(solution)/shard_map/ppermute | solution.py:326
  98.3 2.7 %collective-permute-start.24 = (f32[32,1024]{1,0:T(8,128)S(1)}, f32[32,1024]{1,0:T(8,128)S(1)}, u32[]{:S(2)}, u32[]{:S(2)}) collective-permute-start(f32[32,1024]{1,0:T(8,128)S(1)} %slice.45), channel_id=1, source_target_pairs={{0,224},{32,0},{64,32},{96,64},{128,96},{160,128},{192,160},{224,1... | collective-permute-start | bytes 393224 | tf_op jit(solution)/shard_map/ppermute | solution.py:326
  104.8 2.7 %forward.3 = f32[256,128]{1,0:T(8,128)S(1)} custom-call(f32[64,1024]{1,0:T(8,128)S(1)} %constant_dynamic-update-slice_fusion.refs_0_, f32[64,1024]{1,0:T(8,128)S(1)} %smooth.1.refs_1_, f32[64,1024]{1,0:T(8,128)S(1)} %collective-permute-done.23.refs_2_, f32[64,1024]{1,0:T(8,128)S(1)} %collective-permute-done.19.refs_3_, ...), custom_call_target="tpu_custom_call" | custom-call | tf_op jit(solution)/shard_map/forward/pallas_call | solution.py:271
  110.3 2.7 %forward.2 = f32[256,128]{1,0:T(8,128)S(1)} custom-call(f32[64,1024]{1,0:T(8,128)S(1)} %constant_dynamic-update-slice_fusion.refs_0_, f32[64,1024]{1,0:T(8,128)S(1)} %smooth.1.refs_1_, f32[64,1024]{1,0:T(8,128)S(1)} %collective-permute-done.23.refs_2_, f32[64,1024]{1,0:T(8,128)S(1)} %collective-permute-done.19.refs_3_, ...), custom_call_target="tpu_custom_call" | custom-call | tf_op jit(solution)/shard_map/forward/pallas_call | solution.py:271
  113.1 23.2 %all_to_all.5 = f32[16,16,128]{2,1,0:T(8,128)S(1)} all-to-all(f32[16,16,128]{2,1,0:T(8,128)S(1)} %bitcast.50), channel_id=1, replica_groups=mesh['z'=8,'yl'=2,'x'=4,'yh'=2,'c'=2] {'x','yh','c'}, dimensions={0} | all-to-all | bytes 262144 | tf_op jit(solution)/shard_map/all_to_all | solution.py:384
  (77 shorter events, 38.9 us)
Async XLA Ops:
  4.8 4.1 %collective-permute-start.2 = (f32[2,16,128]{2,1,0:T(8,128)S(1)}, f32[2,16,128]{2,1,0:T(8,128)S(1)}, u32[]{:S(2)}, u32[]{:S(2)}) collective-permute-start(f32[2,16,128]{2,1,0:T(8,128)S(1)} %pad_maximum_fusion.5), channel_id=1, source_target_pairs={{0,18},{2,16},{16,2},{18,0},{1,19},{3,17},{17,3},{19,1},{4,22},{6,... | collective-permute-start | bytes 49160 | tf_op jit(solution)/shard_map/ppermute | solution.py:365
  8.9 5.6 %collective-permute-start.3 = (f32[2,2,16,128]{3,2,1,0:T(8,128)S(1)}, f32[2,2,16,128]{3,2,1,0:T(8,128)S(1)}, u32[]{:S(2)}, u32[]{:S(2)}) collective-permute-start(f32[2,2,16,128]{3,2,1,0:T(8,128)S(1)} %pad_maximum_fusion.4), channel_id=1, source_target_pairs={{0,1},{1,0},{2,3},{3,2},{4,5},{5,4},{6,7},{7,6},{8,9},{9,8},{10,11... | collective-permute-start | bytes 98312 | tf_op jit(solution)/shard_map/ppermute | solution.py:20
  17.3 13.2 %collective-permute-start = (f32[1024,128]{1,0:T(8,128)S(1)}, f32[1024,128]{1,0:T(8,128)S(1)}, u32[]{:S(2)}, u32[]{:S(2)}) collective-permute-start(f32[1024,128]{1,0:T(8,128)S(1)} %get-tuple-element.28), channel_id=1, source_target_pairs={{0,16},{16,0},{1,17},{17,1},{2,18},{18,2},{3,19},{19,3},{4,20},{20... | collective-permute-start | bytes 1572872 | tf_op jit(solution)/shard_map/ppermute | solution.py:20
  17.8 5.3 %collective-permute-start.5 = (f32[2,2,2,2,16,128]{5,4,3,2,1,0:T(8,128)S(1)}, f32[2,2,2,2,16,128]{5,4,3,2,1,0:T(8,128)S(1)}, u32[]{:S(2)}, u32[]{:S(2)}) collective-permute-start(f32[2,2,2,2,16,128]{5,4,3,2,1,0:T(8,128)S(1)} %copy.23), channel_id=1, source_target_pairs={{0,12},{4,8},{8,4},{12,0},{1,13},{5,9},{9,5},{13,1},{2,14},{6,10},... | collective-permute-start | bytes 393224 | tf_op jit(solution)/shard_map/ppermute | solution.py:376
  19.0 23.2 %collective-permute-start.6 = (f32[1024,128]{1,0:T(8,128)S(1)}, f32[1024,128]{1,0:T(8,128)S(1)}, u32[]{:S(2)}, u32[]{:S(2)}) collective-permute-start(f32[1024,128]{1,0:T(8,128)S(1)} %get-tuple-element.39), channel_id=1, source_target_pairs={{0,16},{16,0},{1,17},{17,1},{2,18},{18,2},{3,19},{19,3},{4,20},{20... | collective-permute-start | bytes 1572872 | tf_op jit(solution)/shard_map/ppermute | solution.py:20
  33.1 11.6 %collective-permute-start.13 = (f32[32,1024]{1,0:T(8,128)S(1)}, f32[32,1024]{1,0:T(8,128)S(1)}, u32[]{:S(2)}, u32[]{:S(2)}) collective-permute-start(f32[32,1024]{1,0:T(8,128)S(1)} %get-tuple-element.52), channel_id=1, source_target_pairs={{0,224},{32,0},{64,32},{96,64},{128,96},{160,128},{192,160},{224,1... | collective-permute-start | bytes 393224 | tf_op jit(solution)/shard_map/ppermute | solution.py:326
  37.9 6.8 %collective-permute-start.7 = (f32[32,1024]{1,0:T(8,128)S(1)}, f32[32,1024]{1,0:T(8,128)S(1)}, u32[]{:S(2)}, u32[]{:S(2)}) collective-permute-start(f32[32,1024]{1,0:T(8,128)S(1)} %get-tuple-element.51), channel_id=1, source_target_pairs={{0,32},{32,64},{64,96},{96,128},{128,160},{160,192},{192,224},{224... | collective-permute-start | bytes 393224 | tf_op jit(solution)/shard_map/ppermute | solution.py:326
  40.6 11.4 %collective-permute-start.9 = (f32[1024,128]{1,0:T(8,128)S(1)}, f32[1024,128]{1,0:T(8,128)S(1)}, u32[]{:S(2)}, u32[]{:S(2)}) collective-permute-start(f32[1024,128]{1,0:T(8,128)S(1)} %get-tuple-element.42), channel_id=1, source_target_pairs={{0,16},{16,0},{1,17},{17,1},{2,18},{18,2},{3,19},{19,3},{4,20},{20... | collective-permute-start | bytes 1572872 | tf_op jit(solution)/shard_map/ppermute | solution.py:20
  40.8 21.8 %collective-permute-start.11 = (f32[1024,128]{1,0:T(8,128)S(1)}, f32[1024,128]{1,0:T(8,128)S(1)}, u32[]{:S(2)}, u32[]{:S(2)}) collective-permute-start(f32[1024,128]{1,0:T(8,128)S(1)} %get-tuple-element.44), channel_id=1, source_target_pairs={{0,16},{16,0},{1,17},{17,1},{2,18},{18,2},{3,19},{19,3},{4,20},{20... | collective-permute-start | bytes 1572872 | tf_op jit(solution)/shard_map/ppermute | solution.py:20
  44.8 9.8 %collective-permute-start.8 = (f32[64,1024]{1,0:T(8,128)S(1)}, f32[64,1024]{1,0:T(8,128)S(1)}, u32[]{:S(2)}, u32[]{:S(2)}) collective-permute-start(f32[64,1024]{1,0:T(8,128)S(1)} %pad_maximum_fusion), channel_id=1, source_target_pairs={{0,32},{32,64},{64,96},{96,128},{128,160},{160,192},{192,224},{224... | collective-permute-start | bytes 786440 | tf_op jit(solution)/shard_map/ppermute | solution.py:326
  45.3 11.2 %collective-permute-start.14 = (f32[64,1024]{1,0:T(8,128)S(1)}, f32[64,1024]{1,0:T(8,128)S(1)}, u32[]{:S(2)}, u32[]{:S(2)}) collective-permute-start(f32[64,1024]{1,0:T(8,128)S(1)} %pad_maximum_fusion.1), channel_id=1, source_target_pairs={{0,224},{32,0},{64,32},{96,64},{128,96},{160,128},{192,160},{224,1... | collective-permute-start | bytes 786440 | tf_op jit(solution)/shard_map/ppermute | solution.py:326
  54.6 10.5 %collective-permute-start.10 = (f32[64,1024]{1,0:T(8,128)S(1)}, f32[64,1024]{1,0:T(8,128)S(1)}, u32[]{:S(2)}, u32[]{:S(2)}) collective-permute-start(f32[64,1024]{1,0:T(8,128)S(1)} %add.28), channel_id=1, source_target_pairs={{0,32},{32,64},{64,96},{96,128},{128,160},{160,192},{192,224},{224... | collective-permute-start | bytes 786440 | tf_op jit(solution)/shard_map/ppermute | solution.py:326
  56.5 11.2 %collective-permute-start.15 = (f32[64,1024]{1,0:T(8,128)S(1)}, f32[64,1024]{1,0:T(8,128)S(1)}, u32[]{:S(2)}, u32[]{:S(2)}) collective-permute-start(f32[64,1024]{1,0:T(8,128)S(1)} %add.32), channel_id=1, source_target_pairs={{0,224},{32,0},{64,32},{96,64},{128,96},{160,128},{192,160},{224,1... | collective-permute-start | bytes 786440 | tf_op jit(solution)/shard_map/ppermute | solution.py:326
  65.1 9.8 %collective-permute-start.12 = (f32[64,1024]{1,0:T(8,128)S(1)}, f32[64,1024]{1,0:T(8,128)S(1)}, u32[]{:S(2)}, u32[]{:S(2)}) collective-permute-start(f32[64,1024]{1,0:T(8,128)S(1)} %add.29), channel_id=1, source_target_pairs={{0,32},{32,64},{64,96},{96,128},{128,160},{160,192},{192,224},{224... | collective-permute-start | bytes 786440 | tf_op jit(solution)/shard_map/ppermute | solution.py:326
  67.8 7.2 %collective-permute-start.16 = (f32[64,1024]{1,0:T(8,128)S(1)}, f32[64,1024]{1,0:T(8,128)S(1)}, u32[]{:S(2)}, u32[]{:S(2)}) collective-permute-start(f32[64,1024]{1,0:T(8,128)S(1)} %add.33), channel_id=1, source_target_pairs={{0,224},{32,0},{64,32},{96,64},{128,96},{160,128},{192,160},{224,1... | collective-permute-start | bytes 786440 | tf_op jit(solution)/shard_map/ppermute | solution.py:326
  77.2 6.5 %collective-permute-start.17 = (f32[64,1024]{1,0:T(8,128)S(1)}, f32[64,1024]{1,0:T(8,128)S(1)}, u32[]{:S(2)}, u32[]{:S(2)}) collective-permute-start(f32[64,1024]{1,0:T(8,128)S(1)} %smooth.1.refs_1_), channel_id=1, source_target_pairs={{0,32},{32,64},{64,96},{96,128},{128,160},{160,192},{192,224},{224... | collective-permute-start | bytes 786440 | tf_op jit(solution)/shard_map/ppermute | solution.py:326
  77.9 7.4 %collective-permute-start.21 = (f32[64,1024]{1,0:T(8,128)S(1)}, f32[64,1024]{1,0:T(8,128)S(1)}, u32[]{:S(2)}, u32[]{:S(2)}) collective-permute-start(f32[64,1024]{1,0:T(8,128)S(1)} %smooth.1.refs_1_), channel_id=1, source_target_pairs={{0,224},{32,0},{64,32},{96,64},{128,96},{160,128},{192,160},{224,1... | collective-permute-start | bytes 786440 | tf_op jit(solution)/shard_map/ppermute | solution.py:326
  83.7 6.4 %collective-permute-start.18 = (f32[64,1024]{1,0:T(8,128)S(1)}, f32[64,1024]{1,0:T(8,128)S(1)}, u32[]{:S(2)}, u32[]{:S(2)}) collective-permute-start(f32[64,1024]{1,0:T(8,128)S(1)} %collective-permute-done.17.refs_3_), channel_id=1, source_target_pairs={{0,32},{32,64},{64,96},{96,128},{128,160},{160,192},{192,224},{224... | collective-permute-start | bytes 786440 | tf_op jit(solution)/shard_map/ppermute | solution.py:326
  85.3 5.9 %collective-permute-start.22 = (f32[64,1024]{1,0:T(8,128)S(1)}, f32[64,1024]{1,0:T(8,128)S(1)}, u32[]{:S(2)}, u32[]{:S(2)}) collective-permute-start(f32[64,1024]{1,0:T(8,128)S(1)} %collective-permute-done.21.refs_2_), channel_id=1, source_target_pairs={{0,224},{32,0},{64,32},{96,64},{128,96},{160,128},{192,160},{224,1... | collective-permute-start | bytes 786440 | tf_op jit(solution)/shard_map/ppermute | solution.py:326
  90.1 7.8 %collective-permute-start.19 = (f32[64,1024]{1,0:T(8,128)S(1)}, f32[64,1024]{1,0:T(8,128)S(1)}, u32[]{:S(2)}, u32[]{:S(2)}) collective-permute-start(f32[64,1024]{1,0:T(8,128)S(1)} %collective-permute-done.18.refs_1_), channel_id=1, source_target_pairs={{0,32},{32,64},{64,96},{96,128},{128,160},{160,192},{192,224},{224... | collective-permute-start | bytes 786440 | tf_op jit(solution)/shard_map/ppermute | solution.py:326
  91.1 7.1 %collective-permute-start.23 = (f32[64,1024]{1,0:T(8,128)S(1)}, f32[64,1024]{1,0:T(8,128)S(1)}, u32[]{:S(2)}, u32[]{:S(2)}) collective-permute-start(f32[64,1024]{1,0:T(8,128)S(1)} %collective-permute-done.22.refs_0_), channel_id=1, source_target_pairs={{0,224},{32,0},{64,32},{96,64},{128,96},{160,128},{192,160},{224,1... | collective-permute-start | bytes 786440 | tf_op jit(solution)/shard_map/ppermute | solution.py:326
  98.0 6.8 %collective-permute-start.20 = (f32[32,1024]{1,0:T(8,128)S(1)}, f32[32,1024]{1,0:T(8,128)S(1)}, u32[]{:S(2)}, u32[]{:S(2)}) collective-permute-start(f32[32,1024]{1,0:T(8,128)S(1)} %slice.44), channel_id=1, source_target_pairs={{0,32},{32,64},{64,96},{96,128},{128,160},{160,192},{192,224},{224... | collective-permute-start | bytes 393224 | tf_op jit(solution)/shard_map/ppermute | solution.py:326
  98.3 6.5 %collective-permute-start.24 = (f32[32,1024]{1,0:T(8,128)S(1)}, f32[32,1024]{1,0:T(8,128)S(1)}, u32[]{:S(2)}, u32[]{:S(2)}) collective-permute-start(f32[32,1024]{1,0:T(8,128)S(1)} %slice.45), channel_id=1, source_target_pairs={{0,224},{32,0},{64,32},{96,64},{128,96},{160,128},{192,160},{224,1... | collective-permute-start | bytes 393224 | tf_op jit(solution)/shard_map/ppermute | solution.py:326
  107.5 5.5 %collective-permute-start.25 = (f32[256,128]{1,0:T(8,128)S(1)}, f32[256,128]{1,0:T(8,128)S(1)}, u32[]{:S(2)}, u32[]{:S(2)}) collective-permute-start(f32[256,128]{1,0:T(8,128)S(1)} %forward.3), channel_id=1, source_target_pairs={{0,16},{16,0},{1,17},{17,1},{2,18},{18,2},{3,19},{19,3},{4,20},{20... | collective-permute-start | bytes 393224 | tf_op jit(solution)/shard_map/ppermute | solution.py:20
  (3 other events, 17.0 us)
